TPU v7x, 32 devices: a whole 2x2x4 slice. The times are simulated.
32 devices in a mesh: replica: 4 (over y, core), kvhead: 4 (over z), ffn: 2 (over x).
Axes of the slice: x: 2, y: 2, z: 4, core: 2. Of those that a mesh axis runs over, the one named last changes fastest.
Arguments:
- queries: bfloat16 [16, 16384], P('replica', 'kvhead'), may hold values from -400 to 400
- k_cache: bfloat16 [512, 64, 1024], P(('replica', 'ffn'), None, 'kvhead'), may hold values from -6 to 6
- v_cache: bfloat16 [512, 64, 1024], P(('replica', 'ffn'), None, 'kvhead'), may hold values from -6 to 6
- page_table: int32 [16, 32], P('replica', 'ffn'), may hold values from 0 to 63, as said below
- seq_lens: int32 [16], P('replica'), may hold values from 1 to 2048, as said below
- out_proj: bfloat16 [16384, 16384], P('kvhead', ('replica', 'ffn')), may hold values from -0.125 to 0.125
- residual: bfloat16 [16, 16384], P('kvhead', ('replica', 'ffn')), may hold values from -40 to 40
- norm_gain: bfloat16 [16384], P(('replica', 'ffn')), may hold values from 0.099609375 to 1.8984375
- gate_weight: bfloat16 [26624, 16384], P(('replica', 'kvhead', 'ffn')), may hold values from -0.046875 to 0.046875
- up_weight: bfloat16 [26624, 16384], P(('replica', 'kvhead', 'ffn')), may hold values from -0.046875 to 0.046875
Outputs:
- post_attn: bfloat16 [16, 16384], P('kvhead', ('replica', 'ffn'))
- hidden: bfloat16 [16, 26624], P(None, ('replica', 'kvhead', 'ffn'))
Inputs may be any that keep to these rules, and one draw needn't show every extreme that they name: `page_table`: over the 4 rows of one replica, the entries of page columns j with the same j // 16 name every pool page 0 to 63 exactly once. `seq_lens`: some row has length 2048.
All inputs are finite; a program needn't handle non-finite values.
Results may differ from a plain program's by a relative error of at most 0.0079.
Values may be sent and summed in bfloat16 or wider, within the bound.
A program may use at most 192 MiB of HBM per device.

v0:
```python
import math

import jax
import jax.numpy as jnp
from jax import lax
from jax.sharding import PartitionSpec as P

D = 16384
HD = 128
GQ = 16


NEG_FILL = -1e30
NORM_EPS = 1e-05


def merged(part, axis, combine):
    gathered = jax.tree.map(lambda a: lax.all_gather(a, axis), part)

    def take(source):
        return jax.tree.map(lambda a: lax.dynamic_index_in_dim(a, source, 0, False), gathered)

    return lax.fori_loop(
        1, lax.axis_size(axis), lambda source, state: combine(state, take(source)), take(0)
    )


def join_parts(earlier, later):
    first_max, first_total, first_out = earlier
    second_max, second_total, second_out = later
    overall = jnp.maximum(first_max, second_max)
    first_factor = jnp.exp(first_max - overall)
    second_factor = jnp.exp(second_max - overall)
    joined_total = first_total * first_factor + second_total * second_factor
    joined_out = first_out * first_factor[..., None] + second_out * second_factor[..., None]
    return (overall, joined_total, joined_out)


def per_device(
    queries,
    k_cache,
    v_cache,
    page_table,
    seq_lens,
    out_proj,
    residual,
    norm_gain,
    gate_weight,
    up_weight,
):
    score_scale = 1.0 / math.sqrt(HD)
    row_count = queries.shape[0]
    local_heads = k_cache.shape[2] // HD
    span_len = page_table.shape[1] * k_cache.shape[1]
    key_rows = k_cache[page_table].reshape(row_count, span_len, local_heads, HD)
    value_rows = v_cache[page_table].reshape(row_count, span_len, local_heads, HD)
    query_heads = queries.reshape(row_count, local_heads, GQ, HD)
    scores = (
        jnp.einsum("rkgd,rskd->rkgs", query_heads, key_rows, preferred_element_type=jnp.float32)
        * score_scale
    )
    positions = lax.axis_index("ffn") * span_len + jnp.arange(span_len, dtype=jnp.int32)
    visible = (positions[None, :] < seq_lens[:, None])[:, None, None, :]
    block_max = jnp.max(jnp.where(visible, scores, NEG_FILL), axis=-1)
    weights = jnp.where(visible, jnp.exp(scores - block_max[..., None]), 0.0)
    block_total = jnp.sum(weights, axis=-1)
    block_out = jnp.einsum(
        "rkgs,rskd->rkgd",
        weights.astype(jnp.bfloat16),
        value_rows,
        preferred_element_type=jnp.float32,
    )
    overall, denominator, weighted = merged((block_max, block_total, block_out), "ffn", join_parts)
    contexts = (
        (weighted / denominator[..., None])
        .astype(jnp.bfloat16)
        .reshape(row_count, local_heads * GQ * HD)
    )
    partial_value = jnp.dot(
        lax.all_gather(contexts, "replica", axis=0, tiled=True),
        out_proj,
        preferred_element_type=jnp.float32,
    )
    own_count = residual.shape[0]
    own_first = lax.axis_index("kvhead") * own_count
    own_part = lax.dynamic_slice_in_dim(partial_value, own_first, own_count, 0) + residual.astype(
        jnp.float32
    )
    partial_value = lax.dynamic_update_slice_in_dim(partial_value, own_part, own_first, 0)
    gain_wide = norm_gain.astype(jnp.float32)
    summed = lax.psum(partial_value, "kvhead")
    post_all = summed.astype(jnp.bfloat16)
    post_attn = lax.dynamic_slice_in_dim(post_all, own_first, own_count, 0)
    widened = post_all.astype(jnp.float32)
    squares = lax.psum(jnp.sum(widened * widened, axis=1), ("replica", "ffn"))
    normed = (widened * lax.rsqrt(squares / D + NORM_EPS)[:, None] * gain_wide).astype(jnp.bfloat16)
    contract = (((1,), (1,)), ((), ()))
    shard_cols = lax.all_gather(normed, ("replica", "ffn"), axis=1, tiled=True)
    gate_sum = lax.dot_general(
        shard_cols, gate_weight, contract, preferred_element_type=jnp.float32
    )
    up_sum = lax.dot_general(shard_cols, up_weight, contract, preferred_element_type=jnp.float32)
    hidden = (jax.nn.silu(gate_sum) * up_sum).astype(jnp.bfloat16)
    return (post_attn, hidden)


def solution(mesh):
    in_specs = (
        P("replica", "kvhead"),
        P(("replica", "ffn"), None, "kvhead"),
        P(("replica", "ffn"), None, "kvhead"),
        P("replica", "ffn"),
        P("replica"),
        P("kvhead", ("replica", "ffn")),
        P("kvhead", ("replica", "ffn")),
        P(("replica", "ffn")),
        P(("replica", "kvhead", "ffn"), None),
        P(("replica", "kvhead", "ffn"), None),
    )
    out_specs = (P("kvhead", ("replica", "ffn")), P(None, ("replica", "kvhead", "ffn")))
    return jax.shard_map(
        per_device, mesh=mesh, in_specs=in_specs, out_specs=out_specs, check_vma=False
    )
```

profile of v0, /device:TPU:0, one launch (start us, length us, event | category | flops | bytes accessed | tf_op | source)
XLA Modules:
  0.0 120.8 jit_solution(7688263210400951377)
XLA Ops:
  0.6 0.0 copy-start
  0.7 0.9 broadcast_compare_fusion
  1.5 0.7 compare_select_fusion
  2.2 0.1 reshape.100
  2.3 0.0 copy-done
  2.3 2.0 %gather_fusion = bf16[64,64,256]{2,1,0:T(8,128)(2,1)} fusion(bf16[64,64,256]{2,1,0:T(8,128)(2,1)S(1)} %copy-done, s32[1024]{0:T(1024)S(1)} %pad_clamp_fusion), kind=kCustom, calls=%fused_computation | custom fusion | bytes 4194560 | tf_op jit(solution)/shard_map/gather | solution.py:55
  4.4 2.6 %reshape.95 = bf16[4,1024,2,128]{3,2,1,0:T(2,128)(2,1)S(1)} reshape(bf16[64,64,256]{2,1,0:T(8,128)(2,1)} %gather_fusion) | data formatting | bytes 4194304 | tf_op jit(solution)/shard_map/reshape | solution.py:55
  6.9 0.0 copy-done.2
  6.9 0.7 select_reduce_fusion
  7.7 0.3 bitcast_reduce_fusion
  7.9 5.3 %all-gather.2 = f32[8,2,16]{2,1,0:T(2,128)S(1)} all-gather(f32[4,2,16]{2,1,0:T(2,128)S(1)} %bitcast_reduce_fusion), channel_id=4, replica_groups=mesh['replica'=4,'kvhead'=4,'ffn'=2] {'ffn'}, dimensions={0}, use_global_device_ids=true | all-gather | bytes 1536 | tf_op jit(solution)/shard_map/all_gather | solution.py:18
  13.2 4.3 %all-gather.1 = f32[8,2,16]{2,1,0:T(2,128)S(1)} all-gather(f32[4,2,16]{2,1,0:T(2,128)S(1)} %get-tuple-element.21), channel_id=3, replica_groups=mesh['replica'=4,'kvhead'=4,'ffn'=2] {'ffn'}, dimensions={0}, use_global_device_ids=true | all-gather | bytes 1536 | tf_op jit(solution)/shard_map/all_gather | solution.py:18
  17.6 2.3 %gather_fusion.1 = bf16[64,64,256]{2,1,0:T(8,128)(2,1)S(1)} fusion(bf16[64,64,256]{2,1,0:T(8,128)(2,1)} %param.12, s32[1024]{0:T(1024)S(1)} %pad_clamp_fusion), kind=kCustom, calls=%fused_computation.1 | custom fusion | bytes 4194560 | tf_op jit(solution)/shard_map/gather | solution.py:56
  19.9 2.1 %reshape.97 = bf16[4,1024,2,128]{3,2,1,0:T(2,128)(2,1)} reshape(bf16[64,64,256]{2,1,0:T(8,128)(2,1)S(1)} %gather_fusion.1) | data formatting | bytes 4194304 | tf_op jit(solution)/shard_map/reshape | solution.py:56
  22.0 2.0 %fusion = f32[4,2,16,128]{3,2,1,0:T(8,128)S(1)} fusion(bf16[4,1024,2,128]{3,2,1,0:T(2,128)(2,1)} %reshape.97, f32[4,2,1024,16]{2,3,1,0:T(8,128)S(1)} %get-tuple-element.22, f32[4,2,16]{2,1,0:T(2,128)S(1)} %get-tuple-element.21, pred[4,1024]{1,0:T(4,128)(4,1)S(1)} %broadcast_compare_fusion), kind=kOutput, calls=%fused_computation.2 | convolution fusion | flops 33947648 | bytes 2691584 | tf_op jit(solution)/shard_map/rkgs,rskd->rkgd/dot_general | solution.py:67
  24.0 4.9 %all-gather = f32[8,2,16,128]{3,2,1,0:T(8,128)S(1)} all-gather(f32[4,2,16,128]{3,2,1,0:T(8,128)S(1)} %fusion), channel_id=2, replica_groups=mesh['replica'=4,'kvhead'=4,'ffn'=2] {'ffn'}, dimensions={0}, use_global_device_ids=true | all-gather | bytes 196608 | tf_op jit(solution)/shard_map/all_gather | solution.py:18
  28.9 0.1 fusion.16
  29.1 5.6 %all-gather.3 = bf16[4,4,4096]{2,1,0:T(4,128)(2,1)S(1)} all-gather(bf16[1,4,4096]{2,1,0:T(4,128)(2,1)S(1)} %reshape.139), channel_id=1, replica_groups=mesh['replica'=4,'kvhead'=4,'ffn'=2] {'replica'}, dimensions={0}, use_global_device_ids=true | all-gather | bytes 163840 | tf_op jit(solution)/shard_map/all_gather | solution.py:80
  34.7 0.0 copy-start.3
  34.7 0.0 copy-start.4
  34.8 8.1 %fusion.23 = f32[16,2048]{1,0:T(8,128)S(1)} fusion(bf16[16,4096]{1,0:T(8,128)(2,1)S(1)} %reshape.140, bf16[4096,2048]{1,0:T(8,128)(2,1)} %param.15), kind=kOutput, calls=%fused_computation.41 | convolution fusion | flops 268435456 | bytes 17039360 | tf_op jit(solution)/shard_map/dot_general | solution.py:79
  42.8 0.0 copy-done.3
  42.8 21.9 %all-reduce.1 = bf16[16,2048]{1,0:T(8,128)(2,1)S(1)} all-reduce(f32[16,2048]{1,0:T(8,128)S(1)} %add_dynamic-update-slice_fusion), channel_id=1, replica_groups=mesh['replica'=4,'kvhead'=4,'ffn'=2] {'kvhead'}, use_global_device_ids=true, to_apply=%region_2.3 | all-reduce | flops 32768 | bytes 196608 | tf_op jit(solution)/shard_map/psum | solution.py:91
  64.7 0.1 fusion.11
  64.9 13.4 %psum.15 = f32[16]{0:T(128)S(1)} all-reduce(f32[16]{0:T(128)S(1)} %fusion.11), channel_id=1, replica_groups=mesh['replica'=4,'kvhead'=4,'ffn'=2] {'replica','ffn'}, use_global_device_ids=true, to_apply=%region_4.5 | all-reduce | flops 16 | bytes 128 | tf_op jit(solution)/shard_map/psum | solution.py:95
  78.2 0.0 copy-done.4
  78.2 0.1 fusion.13
  78.3 16.3 %all_gather.31 = bf16[16,16384]{1,0:T(8,128)(2,1)S(1)} all-gather(bf16[16,2048]{1,0:T(8,128)(2,1)S(1)} %fusion.13), channel_id=1, replica_groups=mesh['replica'=4,'kvhead'=4,'ffn'=2] {'replica','ffn'}, dimensions={1}, use_global_device_ids=true | all-gather | bytes 589824 | tf_op jit(solution)/shard_map/all_gather | solution.py:98
  94.6 12.4 %fusion.24 = f32[16,832]{1,0:T(8,128)S(1)} fusion(bf16[16,16384]{1,0:T(8,128)(2,1)S(1)} %all_gather.31, bf16[832,16384]{1,0:T(8,128)(2,1)} %param.18), kind=kOutput, calls=%fused_computation.42 | convolution fusion | flops 436207616 | bytes 27840512 | tf_op jit(solution)/shard_map/dot_general | solution.py:99
  107.0 13.2 %fusion.7 = bf16[16,832]{1,0:T(8,128)(2,1)} fusion(bf16[16,16384]{1,0:T(8,128)(2,1)S(1)} %all_gather.31, bf16[832,16384]{1,0:T(8,128)(2,1)} %param.19, f32[16,832]{1,0:T(8,128)S(1)} %fusion.24), kind=kOutput, calls=%fused_computation.8 | convolution fusion | flops 436287488 | bytes 27867136 | tf_op jit(solution)/shard_map/dot_general | solution.py:102
  120.2 0.6 constant_dynamic-slice_fusion
  120.8 0.0 copy-done.1
  (11 shorter events, 0.1 us)
Async XLA Ops:
  0.6 1.7 %copy-start = (bf16[64,64,256]{2,1,0:T(8,128)(2,1)S(1)}, bf16[64,64,256]{2,1,0:T(8,128)(2,1)}, u32[]{:S(2)}) copy-start(bf16[64,64,256]{2,1,0:T(8,128)(2,1)} %param.11) | copy-start | bytes 6291460
  4.4 2.6 %copy-start.2 = (bf16[4,4096]{1,0:T(4,128)(2,1)S(1)}, bf16[4,4096]{1,0:T(4,128)(2,1)}, u32[]{:S(2)}) copy-start(bf16[4,4096]{1,0:T(4,128)(2,1)} %param.10) | copy-start | bytes 98308
  34.7 8.1 %copy-start.3 = (bf16[4,2048]{1,0:T(4,128)(2,1)S(1)}, bf16[4,2048]{1,0:T(4,128)(2,1)}, u32[]{:S(2)}) copy-start(bf16[4,2048]{1,0:T(4,128)(2,1)} %param.16) | copy-start | bytes 49156
  34.7 43.5 %copy-start.4 = (bf16[2048]{0:T(1024)(128)(2,1)S(1)}, bf16[2048]{0:T(1024)(128)(2,1)}, u32[]{:S(2)}) copy-start(bf16[2048]{0:T(1024)(128)(2,1)} %param.17) | copy-start | bytes 12292
  107.0 13.8 %copy-start.1 = (bf16[64,64,256]{2,1,0:T(8,128)(2,1)S(1)}, bf16[64,64,256]{2,1,0:T(8,128)(2,1)}, u32[]{:S(2)}) copy-start(bf16[64,64,256]{2,1,0:T(8,128)(2,1)} %param.11) | copy-start | bytes 6291460
where the time goes:
time: 122 us; the launch traced here: 121 us
  blocking collectives  71.7 us (59%)
  matrix products  36.4 us (30%)
  local copies, waits for them, and re-layouts  9.74 us (8%)
  other arithmetic  2.21 us (2%)
    psum x1, blocking collectives, per_device(): summed = lax.psum(partial_value, 'kvhead')  21.9 us
    all_gather x1, blocking collectives, per_device(): shard_cols = lax.all_gather(normed, ('replica', 'ffn'), axis=1, tiled=True)  16.3 us
    all_gather x3, blocking collectives, merged(): gathered = jax.tree.map(lambda a: lax.all_gather(a, axis), part)  14.6 us
    psum x1, blocking collectives, per_device(): squares = lax.psum(jnp.sum(widened * widened, axis=1), ('replica', 'ffn'))  13.4 us
    dot_general x1, matrix products, per_device(): lax.dot_general(shard_cols, up_weight, contract, preferred_element_type=j...  13.2 us
    dot_general x1, matrix products, per_device(): lax.dot_general(shard_cols, gate_weight, contract, preferred_element_type...  12.4 us
    dot_general x1, matrix products, per_device(): jnp.dot(lax.all_gather(contexts, 'replica', axis=0, tiled=True), out_proj...  8.05 us
    all_gather x1, blocking collectives, per_device(): lax.all_gather(contexts, 'replica', axis=0, tiled=True)  5.61 us

commit v1 on v0

--- a/solution.py
+++ b/solution.py
@@ -1,8 +1,11 @@
+import functools
 import math
 
 import jax
 import jax.numpy as jnp
 from jax import lax
+from jax.experimental import pallas as pl
+from jax.experimental.pallas import tpu as pltpu
 from jax.sharding import PartitionSpec as P
 
 D = 16384
@@ -12,6 +15,11 @@
 
 NEG_FILL = -1e30
 NORM_EPS = 1e-05
+MESH = pl.DeviceIdType.MESH
+VMEM_BYTES = 67043328
+F32 = jnp.float32
+BF16 = jnp.bfloat16
+NT = (((1,), (1,)), ((), ()))
 
 
 def merged(part, axis, combine):
@@ -36,7 +44,7 @@
     return (overall, joined_total, joined_out)
 
 
-def per_device(
+def general_path(
     queries,
     k_cache,
     v_cache,
@@ -104,6 +112,428 @@
     return (post_attn, hidden)
 
 
+def layer_kernel(
+    sizes,
+    page_ref,
+    len_ref,
+    query_ref,
+    resid_ref,
+    gain_ref,
+    k_hbm,
+    v_hbm,
+    proj_hbm,
+    gate_hbm,
+    up_hbm,
+    post_ref,
+    hidden_ref,
+    k_buf,
+    v_buf,
+    slots,
+    q_heads,
+    o_heads,
+    stat_cols,
+    stats,
+    ctx_parts,
+    ctx_wide,
+    part,
+    z_parts,
+    blocks,
+    gains,
+    x_buf,
+    gate_acc,
+    up_acc,
+    kv_sem,
+    slot_sem,
+    stat_send,
+    stat_recv,
+    ctx_send,
+    ctx_recv,
+    gain_send,
+    gain_recv,
+    z_send,
+    z_recv,
+    blk_send,
+    blk_recv,
+    fwd_send,
+):
+    n_rep, n_kv, n_ffn, n_slots, proj_rows = sizes
+    replica = lax.axis_index("replica")
+    kvhead = lax.axis_index("kvhead")
+    ffn = lax.axis_index("ffn")
+    rows, width = query_ref.shape
+    heads = width // HD
+    page_len = k_hbm.shape[1]
+    kv_heads = k_hbm.shape[2] // HD
+    pages = page_ref.shape[1]
+    span = pages * page_len
+    depth, cols = proj_hbm.shape
+    all_rows = n_rep * rows
+    own_rows = resid_ref.shape[0]
+    n_chip = n_rep // 2
+    chip, core = replica // 2, replica % 2
+
+    def shard_of(rep, f):
+        return rep * n_ffn + f
+
+    me = shard_of(replica, ffn)
+
+    def send(ref, index, sem_out, sem_in, target):
+        return pltpu.make_async_remote_copy(
+            src_ref=ref.at[index],
+            dst_ref=ref.at[index],
+            send_sem=sem_out,
+            recv_sem=sem_in,
+            device_id=target,
+            device_id_type=MESH,
+        )
+
+    plane = []
+    for a in range(n_chip):
+        for c in range(2):
+            for b in range(n_ffn):
+                if (a, c, b) != (0, 0, 0):
+                    rep = ((chip + a) % n_chip) * 2 + (core + c) % 2
+                    plane.append((rep, (ffn + b) % n_ffn))
+    lines = [(kvhead + k) % n_kv for k in range(1, n_kv)]
+
+    k_copy = pltpu.make_async_copy(k_hbm, k_buf, kv_sem.at[0])
+    v_copy = pltpu.make_async_copy(v_hbm, v_buf, kv_sem.at[1])
+    k_copy.start()
+    v_copy.start()
+    proj_copies = []
+    for i, first in enumerate(range(0, depth, proj_rows)):
+        count = min(proj_rows, depth - first)
+        copy = pltpu.make_async_copy(
+            proj_hbm.at[pl.ds(first, count), :], slots.at[i, pl.ds(0, count), :], slot_sem.at[i]
+        )
+        copy.start()
+        proj_copies.append((copy, first, count))
+    n_proj = len(proj_copies)
+
+    direct = []
+    for a in range(n_chip):
+        for b in range(n_ffn):
+            direct.append((a, b))
+    direct.sort(key=lambda ab: (ab[0] + ab[1], ab[0]))
+    order = [(0, 0, 0), (0, 0, 1)]
+    order += [(a, b, 0) for a, b in direct[1:]] + [(a, b, 1) for a, b in direct[1:]]
+
+    def place(a, b, c):
+        rep = ((chip + a) % n_chip) * 2 + (core + c) % 2
+        return rep, (ffn + b) % n_ffn
+
+    weight_copies = []
+    for step, where in enumerate(order):
+        shard = shard_of(*place(*where))
+        window = pl.ds(pl.multiple_of(shard * cols, cols), cols)
+        for which, source in enumerate((gate_hbm, up_hbm)):
+            slot = (n_proj + 2 * step + which) % n_slots
+            weight_copies.append(
+                pltpu.make_async_copy(source.at[:, window], slots.at[slot, pl.ds(0, source.shape[0]), :], slot_sem.at[slot])
+            )
+    early = n_slots - n_proj
+    for copy in weight_copies[:early]:
+        copy.start()
+
+    barrier = pltpu.get_barrier_semaphore()
+    for rep, f in plane:
+        pl.semaphore_signal(
+            barrier, inc=1, device_id={"replica": rep, "ffn": f}, device_id_type=MESH
+        )
+    for k in lines:
+        pl.semaphore_signal(barrier, inc=1, device_id={"kvhead": k}, device_id_type=MESH)
+
+    for h in range(heads):
+        q_heads[pl.ds(h, rows, stride=heads), :] = query_ref[:, h * HD : (h + 1) * HD].astype(F32)
+    gains[me] = gain_ref[...].astype(F32)
+
+    pl.semaphore_wait(barrier, len(plane) + len(lines))
+
+    gain_copies = []
+    for i, (rep, f) in enumerate(plane):
+        copy = send(gains, me, gain_send.at[i], gain_recv.at[me], {"replica": rep, "ffn": f})
+        copy.start()
+        gain_copies.append(copy)
+
+    scale = 1.0 / math.sqrt(HD)
+    position = ffn * span + lax.broadcasted_iota(jnp.int32, (GQ, span), 1)
+    lane = lax.broadcasted_iota(jnp.int32, (GQ, HD), 1)
+    k_copy.wait()
+    weights = []
+    for r in range(rows):
+        visible = position < len_ref[r]
+        for g in range(kv_heads):
+            keys = jnp.concatenate(
+                [k_buf[page_ref[r, j], :, g * HD : (g + 1) * HD] for j in range(pages)], axis=0
+            )
+            first = (r * kv_heads + g) * GQ
+            query = q_heads[first : first + GQ, :].astype(BF16)
+            scores = lax.dot_general(query, keys, NT, preferred_element_type=F32) * scale
+            top = jnp.max(jnp.where(visible, scores, NEG_FILL), axis=1, keepdims=True)
+            weight = jnp.where(visible, jnp.exp(scores - top), 0.0)
+            total = jnp.sum(weight, axis=1, keepdims=True)
+            stat_cols[first : first + GQ, :] = jnp.where(
+                lane < HD // 2,
+                jnp.broadcast_to(top, (GQ, HD)),
+                jnp.broadcast_to(total, (GQ, HD)),
+            )
+            weights.append(weight.astype(BF16))
+    turned = stat_cols[...].T
+    stats[0, 0:1, :] = turned[0:1, :]
+    stats[0, 1:2, :] = turned[HD // 2 : HD // 2 + 1, :]
+    stat_copy = pltpu.make_async_remote_copy(
+        src_ref=stats.at[0],
+        dst_ref=stats.at[1],
+        send_sem=stat_send,
+        recv_sem=stat_recv,
+        device_id={"ffn": (ffn + 1) % n_ffn},
+        device_id_type=MESH,
+    )
+    stat_copy.start()
+    v_copy.wait()
+    for r in range(rows):
+        for g in range(kv_heads):
+            values = jnp.concatenate(
+                [v_buf[page_ref[r, j], :, g * HD : (g + 1) * HD] for j in range(pages)], axis=0
+            )
+            first = (r * kv_heads + g) * GQ
+            o_heads[first : first + GQ, :] = jnp.dot(
+                weights[r * kv_heads + g], values, preferred_element_type=F32
+            )
+    stat_copy.wait()
+    own_top, own_total = stats[0, 0:1, :], stats[0, 1:2, :]
+    far_top, far_total = stats[1, 0:1, :], stats[1, 1:2, :]
+    overall = jnp.maximum(own_top, far_top)
+    own_lift = jnp.exp(own_top - overall)
+    far_lift = jnp.exp(far_top - overall)
+    factor = own_lift / (own_lift * own_total + far_lift * far_total)
+    o_heads[...] = o_heads[...] * jnp.broadcast_to(factor, (HD, HD)).T
+    for h in range(heads):
+        ctx_parts[me, :, h * HD : (h + 1) * HD] = o_heads[
+            pl.ds(h, rows, stride=heads), :
+        ].astype(BF16)
+    ctx_copies = []
+    for i, (rep, f) in enumerate(plane):
+        copy = send(ctx_parts, me, ctx_send.at[i], ctx_recv.at[me], {"replica": rep, "ffn": f})
+        copy.start()
+        ctx_copies.append(copy)
+    for rep, f in plane:
+        shard = shard_of(rep, f)
+        send(
+            ctx_parts, shard, ctx_send.at[0], ctx_recv.at[shard], {"replica": rep, "ffn": f}
+        ).wait_recv()
+    for rep in range(n_rep):
+        joined = ctx_parts[rep * n_ffn].astype(F32)
+        for f in range(1, n_ffn):
+            joined = joined + ctx_parts[rep * n_ffn + f].astype(F32)
+        ctx_wide[rep * rows : (rep + 1) * rows, :] = joined
+
+    total = None
+    for i, (copy, first, count) in enumerate(proj_copies):
+        copy.wait()
+        term = jnp.dot(
+            ctx_wide[:, first : first + count].astype(BF16),
+            slots[i, 0:count, :],
+            preferred_element_type=F32,
+        )
+        if i == 0:
+            part[...] = term
+        else:
+            part[...] += term
+    for copy in weight_copies[early:]:
+        copy.start()
+    resid = resid_ref[...].astype(F32)
+    for k in range(n_kv):
+        part[k * own_rows : (k + 1) * own_rows, :] += jnp.where(kvhead == k, resid, 0.0)
+    z_parts[kvhead] = part[...].astype(BF16)
+    z_copies = []
+    for i, k in enumerate(lines):
+        copy = send(z_parts, kvhead, z_send.at[i], z_recv.at[kvhead], {"kvhead": k})
+        copy.start()
+        z_copies.append(copy)
+    gate_acc[...] = jnp.zeros_like(gate_acc)
+    up_acc[...] = jnp.zeros_like(up_acc)
+    for copy in gain_copies:
+        copy.wait_send()
+    for rep, f in plane:
+        shard = shard_of(rep, f)
+        send(
+            gains, shard, gain_send.at[0], gain_recv.at[shard], {"replica": rep, "ffn": f}
+        ).wait_recv()
+    for copy in ctx_copies:
+        copy.wait_send()
+    for k in lines:
+        send(z_parts, k, z_send.at[0], z_recv.at[k], {"kvhead": k}).wait_recv()
+        part[...] += z_parts[k].astype(F32)
+    blocks[me] = part[...].astype(BF16)
+    blk_copies = []
+    for i, where in enumerate([(0, 0, 1)] + [(a, b, 0) for a, b in direct[1:]]):
+        rep, f = place(*where)
+        copy = send(blocks, me, blk_send.at[i], blk_recv.at[me], {"replica": rep, "ffn": f})
+        copy.start()
+        blk_copies.append(copy)
+    own_post = jnp.zeros((own_rows, cols), F32)
+    for k in range(n_kv):
+        own_post = own_post + jnp.where(
+            kvhead == k, part[k * own_rows : (k + 1) * own_rows, :], 0.0
+        )
+    post_ref[...] = own_post.astype(BF16)
+
+    def arrive(where):
+        rep, f = place(*where)
+        shard = shard_of(rep, f)
+        send(
+            blocks, shard, blk_send.at[0], blk_recv.at[shard], {"replica": rep, "ffn": f}
+        ).wait_recv()
+
+    fwd_copies = []
+
+    def pass_on(where):
+        arrive(where)
+        shard = shard_of(*place(*where))
+        copy = send(
+            blocks,
+            shard,
+            fwd_send.at[len(fwd_copies)],
+            blk_recv.at[shard],
+            {"replica": chip * 2 + (core + 1) % 2},
+        )
+        copy.start()
+        fwd_copies.append(copy)
+
+    squares = jnp.zeros((all_rows, 1), F32)
+    pending = [(a, b, 0) for a, b in direct[1:]]
+    piece = 512 if cols % 512 == 0 else cols
+    for step, where in enumerate(order):
+        if step >= 1 and pending:
+            pass_on(pending.pop(0))
+            if pending:
+                pass_on(pending.pop(0))
+        if where[2] == 1:
+            arrive(where)
+        shard = shard_of(*place(*where))
+        wide = blocks[shard].astype(F32)
+        squares = squares + jnp.sum(wide * wide, axis=1, keepdims=True)
+        x_buf[...] = (wide * gains[shard]).astype(BF16)
+        weight_copies[2 * step].wait()
+        weight_copies[2 * step + 1].wait()
+        gate_slot = (n_proj + 2 * step) % n_slots
+        up_slot = (n_proj + 2 * step + 1) % n_slots
+
+        def accumulate(i, carry, gate_slot=gate_slot, up_slot=up_slot):
+            window = pl.ds(pl.multiple_of(i * piece, piece), piece)
+            part_x = x_buf[:, window]
+            units = gate_acc.shape[1]
+            gate_acc[...] += lax.dot_general(
+                part_x, slots[gate_slot, 0:units, window], NT, preferred_element_type=F32
+            )
+            up_acc[...] += lax.dot_general(
+                part_x, slots[up_slot, 0:units, window], NT, preferred_element_type=F32
+            )
+            return carry
+
+        lax.fori_loop(0, cols // piece, accumulate, 0)
+    inverse = lax.rsqrt(squares / D + NORM_EPS)
+    gate = gate_acc[...] * inverse
+    hidden_ref[...] = (gate / (1.0 + jnp.exp(-gate)) * (up_acc[...] * inverse)).astype(BF16)
+    for copy in z_copies + blk_copies + fwd_copies:
+        copy.wait_send()
+
+
+def plan(n_rep, n_kv, n_ffn, shapes):
+    queries, k_cache, v_cache, page_table, seq_lens, out_proj, residual, gain, gate, up = shapes
+    depth, cols = out_proj
+    units = gate[0]
+    rows = queries[0]
+    heads = queries[1] // HD
+    if n_ffn != 2 or n_rep % 2 or units % 16 or cols % 256 or rows * heads != HD:
+        return None
+    if gate[1] != n_rep * n_ffn * cols or page_table[0] * page_table[1] != k_cache[0]:
+        return None
+    proj_rows = units // 256 * 256
+    if proj_rows == 0:
+        return None
+    n_slots = 2 * n_rep * n_ffn
+    n_proj = -(-depth // proj_rows)
+    held = n_slots * units * cols * 2 + 4 * math.prod(k_cache)
+    if n_proj > n_slots or held + (4 << 20) > VMEM_BYTES:
+        return None
+    return n_slots, proj_rows
+
+
+def per_device(sizes, *args):
+    (queries, k_cache, v_cache, page_table, seq_lens, out_proj, residual, gain, gate, up) = args
+    n_rep, n_kv, n_ffn = sizes
+    found = plan(n_rep, n_kv, n_ffn, [a.shape for a in args])
+    if found is None:
+        return general_path(*args)
+    n_slots, proj_rows = found
+    rows, width = queries.shape
+    cols = out_proj.shape[1]
+    units = gate.shape[0]
+    all_rows = n_rep * rows
+    shards = n_rep * n_ffn
+    chips = shards // 2
+    vmem = pl.BlockSpec(memory_space=pltpu.VMEM)
+    smem = pl.BlockSpec(memory_space=pltpu.SMEM)
+    hbm = pl.BlockSpec(memory_space=pl.ANY)
+    dma = pltpu.SemaphoreType.DMA
+    return pl.pallas_call(
+        functools.partial(layer_kernel, (n_rep, n_kv, n_ffn, n_slots, proj_rows)),
+        out_shape=(
+            jax.ShapeDtypeStruct(residual.shape, BF16),
+            jax.ShapeDtypeStruct((all_rows, units), BF16),
+        ),
+        in_specs=[smem, smem, vmem, vmem, vmem] + [hbm] * 5,
+        out_specs=(vmem, vmem),
+        scratch_shapes=[
+            pltpu.VMEM(k_cache.shape, BF16),
+            pltpu.VMEM(v_cache.shape, BF16),
+            pltpu.VMEM((n_slots, units, cols), BF16),
+            pltpu.VMEM((HD, HD), F32),
+            pltpu.VMEM((HD, HD), F32),
+            pltpu.VMEM((HD, HD), F32),
+            pltpu.VMEM((2, 8, HD), F32),
+            pltpu.VMEM((shards, rows, width), BF16),
+            pltpu.VMEM((all_rows, width), F32),
+            pltpu.VMEM((all_rows, cols), F32),
+            pltpu.VMEM((n_kv, all_rows, cols), BF16),
+            pltpu.VMEM((shards, all_rows, cols), BF16),
+            pltpu.VMEM((shards, 1, cols), F32),
+            pltpu.VMEM((all_rows, cols), BF16),
+            pltpu.VMEM((all_rows, units), F32),
+            pltpu.VMEM((all_rows, units), F32),
+            dma((2,)),
+            dma((n_slots,)),
+            dma,
+            dma,
+            dma((shards - 1,)),
+            dma((shards,)),
+            dma((shards - 1,)),
+            dma((shards,)),
+            dma((n_kv - 1,)),
+            dma((n_kv,)),
+            dma((chips,)),
+            dma((shards,)),
+            dma((max(chips - 1, 1),)),
+        ],
+        compiler_params=pltpu.CompilerParams(
+            collective_id=0, has_side_effects=True, vmem_limit_bytes=VMEM_BYTES - (1 << 20)
+        ),
+    )(
+        page_table,
+        seq_lens,
+        queries,
+        residual,
+        gain.reshape(1, cols),
+        k_cache,
+        v_cache,
+        out_proj,
+        gate,
+        up,
+    )
+
+
 def solution(mesh):
     in_specs = (
         P("replica", "kvhead"),
@@ -118,6 +548,11 @@
         P(("replica", "kvhead", "ffn"), None),
     )
     out_specs = (P("kvhead", ("replica", "ffn")), P(None, ("replica", "kvhead", "ffn")))
+    sizes = (mesh.shape["replica"], mesh.shape["kvhead"], mesh.shape["ffn"])
     return jax.shard_map(
-        per_device, mesh=mesh, in_specs=in_specs, out_specs=out_specs, check_vma=False
-    )
+        functools.partial(per_device, sizes),
+        mesh=mesh,
+        in_specs=in_specs,
+        out_specs=out_specs,
+        check_vma=False,
+    )

time: 122 us -> 61.9 us (0.51)
  blocking collectives: 71.7 us -> 0 us
  Pallas kernels: 0 us -> 57 us
  matrix products: 36.4 us -> 0 us
  local copies, waits for them, and re-layouts: 9.74 us -> 3.98 us
  other arithmetic: 2.21 us -> 0 us
    pallas_call x0 -> x1, Pallas kernels: none -> 57 us  [per_device(): pl.pallas_call(functools.partial(layer_kernel, (n_rep, n_kv, n_ffn, n_slo...]
    all_gather x5 -> x0, blocking collectives: 36.5 us -> none  [the longest x1 16.3 us: per_device(): shard_cols = lax.all_gather(normed, ('replica', 'ffn'), axis=1, tiled=True)]
    dot_general x5 -> x0, matrix products: 36.4 us -> none  [the longest x1 13.2 us: per_device(): lax.dot_general(shard_cols, up_weight, contract, preferred_element_type=j...]
    psum x2 -> x0, blocking collectives: 35.2 us -> none  [the longest x1 21.9 us: per_device(): summed = lax.psum(partial_value, 'kvhead')]
    gather x2 -> x0, local copies, waits for them, and re-layouts: 4.31 us -> none  [the longest x1 2.27 us: per_device(): v_cache[page_table].reshape(row_count, span_len, local_heads, HD)]
    reshape x2 -> x1, local copies, waits for them, and re-layouts: 4.64 us -> 1.29 us  [per_device(): gain.reshape(1, cols)]
    unnamed x13 -> x2, local copies, waits for them, and re-layouts: 0.09 us -> 2.69 us
where the time goes in v1:
time: 61.9 us; the launch traced here: 61.6 us
  Pallas kernels  57 us (92%)
  local copies, waits for them, and re-layouts  3.98 us (6%)
  between operations  0.64 us (1%)
    pallas_call x1, Pallas kernels, per_device(): pl.pallas_call(functools.partial(layer_kernel, (n_rep, n_kv, n_ffn, n_slo...  57 us
    unnamed x2, local copies, waits for them, and re-layouts  2.69 us
    reshape x1, local copies, waits for them, and re-layouts, per_device(): gain.reshape(1, cols)  1.29 us

profile of v1, /device:TPU:0, one launch (start us, length us, event | category | flops | bytes accessed | tf_op | source)
XLA Modules:
  0.0 61.6 jit_solution(584575880518526307)
XLA Ops:
  0.6 1.3 %reshape.7.gain_ref = bf16[1,2048]{1,0:T(2,128)(2,1)} reshape(bf16[2048]{0:T(1024)(128)(2,1)} %param.17) | data formatting | bytes 8192 | tf_op jit(solution)/shard_map/reshape | solution.py:528
  1.9 57.0 %shard_map.113 = (bf16[4,2048]{1,0:T(4,128)(2,1)}, bf16[16,832]{1,0:T(8,128)(2,1)}) custom-call(s32[4,16]{1,0:T(4,128)} %page_ref.1, s32[4]{0:T(128)} %len_ref.1, bf16[4,4096]{1,0:T(4,128)(2,1)} %query_ref.1, bf16[4,2048]{1,0:T(4,128)(2,1)} %resid_ref.1, bf16[1,2048]{1,0:T(2,128)(2,1)} %reshape.7.gain_ref, bf16[64,64,256]{2,1,0:T(8,128)(2,1)} %k_hbm.1, ...), custom_call_target="tpu_custom_call" | custom-call | tf_op jit(solution)/shard_map/pallas_call | solution.py:481
  58.9 1.3 %copy.14 = bf16[4,2048]{1,0:T(4,128)(2,1)} copy(bf16[4,2048]{1,0:T(4,128)(2,1)} %get-tuple-element.4) | data formatting | bytes 32768
  60.2 1.4 %copy.15 = bf16[16,832]{1,0:T(8,128)(2,1)} copy(bf16[16,832]{1,0:T(8,128)(2,1)} %get-tuple-element.5) | data formatting | bytes 53248

commit v2 on v1

--- a/solution.py
+++ b/solution.py
@@ -206,7 +206,6 @@
         copy = pltpu.make_async_copy(
             proj_hbm.at[pl.ds(first, count), :], slots.at[i, pl.ds(0, count), :], slot_sem.at[i]
         )
-        copy.start()
         proj_copies.append((copy, first, count))
     n_proj = len(proj_copies)
 
@@ -232,8 +231,7 @@
                 pltpu.make_async_copy(source.at[:, window], slots.at[slot, pl.ds(0, source.shape[0]), :], slot_sem.at[slot])
             )
     early = n_slots - n_proj
-    for copy in weight_copies[:early]:
-        copy.start()
+    opening = min(4, early)
 
     barrier = pltpu.get_barrier_semaphore()
     for rep, f in plane:
@@ -245,7 +243,7 @@
 
     for h in range(heads):
         q_heads[pl.ds(h, rows, stride=heads), :] = query_ref[:, h * HD : (h + 1) * HD].astype(F32)
-    gains[me] = gain_ref[...].astype(F32)
+    gains[me] = gain_ref[...].astype(F32).reshape(1, cols)
 
     pl.semaphore_wait(barrier, len(plane) + len(lines))
 
@@ -259,6 +257,8 @@
     position = ffn * span + lax.broadcasted_iota(jnp.int32, (GQ, span), 1)
     lane = lax.broadcasted_iota(jnp.int32, (GQ, HD), 1)
     k_copy.wait()
+    for copy, _, _ in proj_copies:
+        copy.start()
     weights = []
     for r in range(rows):
         visible = position < len_ref[r]
@@ -317,6 +317,8 @@
         copy = send(ctx_parts, me, ctx_send.at[i], ctx_recv.at[me], {"replica": rep, "ffn": f})
         copy.start()
         ctx_copies.append(copy)
+    for copy in weight_copies[:opening]:
+        copy.start()
     for rep, f in plane:
         shard = shard_of(rep, f)
         send(
@@ -328,29 +330,44 @@
             joined = joined + ctx_parts[rep * n_ffn + f].astype(F32)
         ctx_wide[rep * rows : (rep + 1) * rows, :] = joined
 
-    total = None
-    for i, (copy, first, count) in enumerate(proj_copies):
-        copy.wait()
-        term = jnp.dot(
-            ctx_wide[:, first : first + count].astype(BF16),
-            slots[i, 0:count, :],
-            preferred_element_type=F32,
-        )
-        if i == 0:
-            part[...] = term
+    resid = resid_ref[...].astype(F32)
+    half = cols // 2
+    z_copies = []
+    for side in range(2):
+        window = slice(side * half, (side + 1) * half)
+        for i, (copy, first, count) in enumerate(proj_copies):
+            if side == 0:
+                copy.wait()
+            term = jnp.dot(
+                ctx_wide[:, first : first + count].astype(BF16),
+                slots[i, 0:count, window],
+                preferred_element_type=F32,
+            )
+            if i == 0:
+                part[:, window] = term
+            else:
+                part[:, window] += term
+        if side == 0:
+            for copy in weight_copies[opening:early]:
+                copy.start()
         else:
-            part[...] += term
-    for copy in weight_copies[early:]:
-        copy.start()
-    resid = resid_ref[...].astype(F32)
-    for k in range(n_kv):
-        part[k * own_rows : (k + 1) * own_rows, :] += jnp.where(kvhead == k, resid, 0.0)
-    z_parts[kvhead] = part[...].astype(BF16)
-    z_copies = []
-    for i, k in enumerate(lines):
-        copy = send(z_parts, kvhead, z_send.at[i], z_recv.at[kvhead], {"kvhead": k})
-        copy.start()
-        z_copies.append(copy)
+            for copy in weight_copies[early:]:
+                copy.start()
+        for k in range(n_kv):
+            part[k * own_rows : (k + 1) * own_rows, window] += jnp.where(
+                kvhead == k, resid[:, window], 0.0
+            )
+        z_parts[kvhead, side] = part[:, window].astype(BF16)
+        for i, k in enumerate(lines):
+            copy = send(
+                z_parts,
+                (kvhead, side),
+                z_send.at[side, i],
+                z_recv.at[side, kvhead],
+                {"kvhead": k},
+            )
+            copy.start()
+            z_copies.append(copy)
     gate_acc[...] = jnp.zeros_like(gate_acc)
     up_acc[...] = jnp.zeros_like(up_acc)
     for copy in gain_copies:
@@ -362,9 +379,12 @@
         ).wait_recv()
     for copy in ctx_copies:
         copy.wait_send()
-    for k in lines:
-        send(z_parts, k, z_send.at[0], z_recv.at[k], {"kvhead": k}).wait_recv()
-        part[...] += z_parts[k].astype(F32)
+    for side in range(2):
+        for k in lines:
+            send(
+                z_parts, (k, side), z_send.at[side, 0], z_recv.at[side, k], {"kvhead": k}
+            ).wait_recv()
+            part[:, side * half : (side + 1) * half] += z_parts[k, side].astype(F32)
     blocks[me] = part[...].astype(BF16)
     blk_copies = []
     for i, where in enumerate([(0, 0, 1)] + [(a, b, 0) for a, b in direct[1:]]):
@@ -497,7 +517,7 @@
             pltpu.VMEM((shards, rows, width), BF16),
             pltpu.VMEM((all_rows, width), F32),
             pltpu.VMEM((all_rows, cols), F32),
-            pltpu.VMEM((n_kv, all_rows, cols), BF16),
+            pltpu.VMEM((n_kv, 2, all_rows, cols // 2), BF16),
             pltpu.VMEM((shards, all_rows, cols), BF16),
             pltpu.VMEM((shards, 1, cols), F32),
             pltpu.VMEM((all_rows, cols), BF16),
@@ -511,8 +531,8 @@
             dma((shards,)),
             dma((shards - 1,)),
             dma((shards,)),
-            dma((n_kv - 1,)),
-            dma((n_kv,)),
+            dma((2, n_kv - 1)),
+            dma((2, n_kv)),
             dma((chips,)),
             dma((shards,)),
             dma((max(chips - 1, 1),)),
@@ -525,7 +545,7 @@
         seq_lens,
         queries,
         residual,
-        gain.reshape(1, cols),
+        gain,
         k_cache,
         v_cache,
         out_proj,

time: 61.9 us -> 47.7 us (0.77)
  Pallas kernels: 57 us -> 44.1 us
  local copies, waits for them, and re-layouts: 3.98 us -> 2.69 us
    pallas_call x1, Pallas kernels: 57 us -> 44.1 us  [per_device(): pl.pallas_call(functools.partial(layer_kernel, (n_rep, n_kv, n_ffn, n_slo...]
    reshape x1 -> x0, local copies, waits for them, and re-layouts: 1.29 us -> none  [per_device(): gain.reshape(1, cols)]
where the time goes in v2:
time: 47.7 us; the launch traced here: 47.4 us
  Pallas kernels  44.1 us (92%)
  local copies, waits for them, and re-layouts  2.69 us (6%)
  between operations  0.64 us (1%)
    pallas_call x1, Pallas kernels, per_device(): pl.pallas_call(functools.partial(layer_kernel, (n_rep, n_kv, n_ffn, n_slo...  44.1 us
    unnamed x2, local copies, waits for them, and re-layouts  2.69 us

profile of v2, /device:TPU:0, one launch (start us, length us, event | category | flops | bytes accessed | tf_op | source)
XLA Modules:
  0.0 47.4 jit_solution(3369797842298886345)
XLA Ops:
  0.6 44.1 %shard_map.113 = (bf16[4,2048]{1,0:T(4,128)(2,1)}, bf16[16,832]{1,0:T(8,128)(2,1)}) custom-call(s32[4,16]{1,0:T(4,128)} %page_ref.1, s32[4]{0:T(128)} %len_ref.1, bf16[4,4096]{1,0:T(4,128)(2,1)} %query_ref.1, bf16[4,2048]{1,0:T(4,128)(2,1)} %resid_ref.1, bf16[2048]{0:T(1024)(128)(2,1)} %gain_ref.1, bf16[64,64,256]{2,1,0:T(8,128)(2,1)} %k_hbm.1, ...), custom_call_target="tpu_custom_call" | custom-call | tf_op jit(solution)/shard_map/pallas_call | solution.py:501
  44.7 1.3 %copy.14 = bf16[4,2048]{1,0:T(4,128)(2,1)} copy(bf16[4,2048]{1,0:T(4,128)(2,1)} %get-tuple-element.4) | data formatting | bytes 32768
  46.1 1.4 %copy.15 = bf16[16,832]{1,0:T(8,128)(2,1)} copy(bf16[16,832]{1,0:T(8,128)(2,1)} %get-tuple-element.5) | data formatting | bytes 53248

commit v3 on v2

--- a/solution.py
+++ b/solution.py
@@ -423,7 +423,7 @@
 
     squares = jnp.zeros((all_rows, 1), F32)
     pending = [(a, b, 0) for a, b in direct[1:]]
-    piece = 512 if cols % 512 == 0 else cols
+    piece = cols
     for step, where in enumerate(order):
         if step >= 1 and pending:
             pass_on(pending.pop(0))

time: 47.7 us -> 45 us (0.943)
  Pallas kernels: 44.1 us -> 41.3 us
    pallas_call x1, Pallas kernels: 44.1 us -> 41.3 us  [per_device(): pl.pallas_call(functools.partial(layer_kernel, (n_rep, n_kv, n_ffn, n_slo...]
where the time goes in v3:
time: 45 us; the launch traced here: 44.6 us
  Pallas kernels  41.3 us (92%)
  local copies, waits for them, and re-layouts  2.69 us (6%)
  between operations  0.64 us (1%)
    pallas_call x1, Pallas kernels, per_device(): pl.pallas_call(functools.partial(layer_kernel, (n_rep, n_kv, n_ffn, n_slo...  41.3 us
    unnamed x2, local copies, waits for them, and re-layouts  2.69 us

profile of v3, /device:TPU:0, one launch (start us, length us, event | category | flops | bytes accessed | tf_op | source)
XLA Modules:
  0.0 44.6 jit_solution(11613092785729990760)
XLA Ops:
  0.6 41.3 %shard_map.113 = (bf16[4,2048]{1,0:T(4,128)(2,1)}, bf16[16,832]{1,0:T(8,128)(2,1)}) custom-call(s32[4,16]{1,0:T(4,128)} %page_ref.1, s32[4]{0:T(128)} %len_ref.1, bf16[4,4096]{1,0:T(4,128)(2,1)} %query_ref.1, bf16[4,2048]{1,0:T(4,128)(2,1)} %resid_ref.1, bf16[2048]{0:T(1024)(128)(2,1)} %gain_ref.1, bf16[64,64,256]{2,1,0:T(8,128)(2,1)} %k_hbm.1, ...), custom_call_target="tpu_custom_call" | custom-call | tf_op jit(solution)/shard_map/pallas_call | solution.py:501
  42.0 1.3 %copy.14 = bf16[4,2048]{1,0:T(4,128)(2,1)} copy(bf16[4,2048]{1,0:T(4,128)(2,1)} %get-tuple-element.4) | data formatting | bytes 32768
  43.3 1.4 %copy.15 = bf16[16,832]{1,0:T(8,128)(2,1)} copy(bf16[16,832]{1,0:T(8,128)(2,1)} %get-tuple-element.5) | data formatting | bytes 53248
